TPU v7x, 512 devices: a whole 4x4x16 slice. The times are simulated.
512 devices in a mesh: blk: 32 (over x, z_lo), rep: 16 (over z_hi, y, core).
Axes of the slice: x: 4, y: 4, z: 16 (z_hi: 2, z_lo: 8; z = z_hi * 8 + z_lo), core: 2. Of those that a mesh axis runs over, the one named last changes fastest.
Arguments:
- signals: bfloat16 [32768, 8192], P('rep', 'blk'), may hold values from -6 to 6
- omega: float32 [32, 5, 256, 256], P('blk', None, 'rep'), may hold values from -1.2 to 3, as said below
- pattern: int32 [32, 5], P('blk'), may hold values from 0 to 31, as said below
Outputs:
- omega_next: float32 [32, 5, 256, 256], P('blk', None, 'rep')
Inputs may be any that keep to these rules, and one draw needn't show every extreme that they name: pattern[i, 0] = i. For two distinct whole numbers A and B from 1 to 15, the same in every row, pattern[i, 1] to pattern[i, 4] are i + A, i - A, i + B and i - B modulo 32 in some order, the same order in every row. Omega is symmetric: omega[i, k] is the transpose of omega[pattern[i, k], k2] where pattern[pattern[i, k], k2] = i. The diagonal entries of omega[i, 0] lie between 1 and 3.
All inputs are finite; a program needn't handle non-finite values.
Results may differ from a plain program's by a relative error of at most 0.0033.
Values may be sent and summed in bfloat16 or wider, within the bound.
A program may use at most 128 MiB of HBM per device.

v0:
```python
import jax
import jax.numpy as jnp
from jax import lax
from jax.sharding import Mesh
from jax.sharding import PartitionSpec as P

STEP_SIZE = 0.5
PENALTY = 0.1
REP = ("zh", "y", "c")


def fine_mesh(mesh):
    return Mesh(mesh.devices.reshape(4, 8, 2, 4, 2), ("x", "zl", "zh", "y", "c"))


def per_device(signals, omega, pattern):
    x_size = lax.axis_size("x")
    zl_size = lax.axis_size("zl")
    team_count = x_size * zl_size
    replica_count = lax.axis_size(REP)
    team_index = lax.axis_index(("x", "zl"))
    replica_index = lax.axis_index(REP)
    slot_count, tile_rows, width = omega.shape[1:]
    time_length = signals.shape[0] * replica_count
    offsets = jnp.mod(pattern[0] - team_index, team_count)
    own = signals.reshape(zl_size, signals.shape[0] // zl_size, width)
    blocks = lax.all_to_all(own, "zl", 0, 0, tiled=True)
    blocks = lax.all_gather(blocks, "x", axis=0, tiled=True)
    panels = lax.all_gather(omega.astype(jnp.bfloat16), REP, axis=2, tiled=True)
    panels = lax.all_gather(panels, "zl", axis=0, tiled=True)
    rows = lax.axis_index("x") * zl_size + jnp.arange(zl_size, dtype=jnp.int32)
    columns = jnp.mod(rows[:, None] + offsets[None, :], team_count)
    gathered = blocks[columns]
    mixed = jnp.einsum(
        "jktc,jkdc->jtd", gathered, panels, preferred_element_type=jnp.float32
    ).astype(jnp.bfloat16)
    left = jnp.einsum("jtd,jktc->jkdc", mixed, gathered, preferred_element_type=jnp.float32)
    own_terms = lax.psum_scatter(left, REP, scatter_dimension=2, tiled=True)
    own_terms = lax.psum_scatter(own_terms, "zl", scatter_dimension=0, tiled=True)[0]
    flipped = lax.all_to_all(own_terms, REP, 2, 1, tiled=True)
    flipped = jnp.swapaxes(flipped, 1, 2)
    match = offsets[None, :] == jnp.mod(team_count - offsets, team_count)[:, None]
    mirror = jnp.argmax(match, axis=1)
    outgoing = flipped[mirror]
    for level in range(team_count.bit_length() - 1):
        step = 1 << level
        route = [((i + step) % team_count, i) for i in range(team_count)]
        shifted = lax.ppermute(outgoing, ("x", "zl"), route)
        chosen = jnp.mod(offsets // step, 2) == 1
        outgoing = jnp.where(chosen[:, None, None], shifted, outgoing)
    gradient = (own_terms + outgoing) / (2.0 * time_length)
    tiles = omega[0]
    column_ids = jnp.arange(width, dtype=jnp.int32)
    row_ids = replica_index * tile_rows + jnp.arange(tile_rows, dtype=jnp.int32)
    diagonal = column_ids[None, :] == row_ids[:, None]
    diagonal = diagonal[None] & (offsets == 0)[:, None, None]
    gradient = gradient - jnp.where(diagonal, 1.0 / jnp.where(diagonal, tiles, 1.0), 0.0)
    value = tiles - STEP_SIZE * gradient
    shrunk = jnp.sign(value) * jnp.maximum(jnp.abs(value) - STEP_SIZE * PENALTY, 0.0)
    return jnp.where(diagonal, value, shrunk)[None]


def solution(mesh):
    return jax.shard_map(
        per_device,
        mesh=fine_mesh(mesh),
        in_specs=(P(REP, ("x", "zl")), P(("x", "zl"), None, REP, None), P(("x", "zl"), None)),
        out_specs=P(("x", "zl"), None, REP, None),
        check_vma=False,
    )
```

profile of v0, /device:TPU:230, one launch (start us, length us, event | category | flops | bytes accessed | tf_op | source)
XLA Modules:
  0.0 669.5 jit_solution(8638916152552195182)
XLA Ops:
  6.5 55.6 %all_to_all.23 = bf16[8,256,256]{2,1,0:T(8,128)(2,1)} all-to-all(bf16[8,256,256]{2,1,0:T(8,128)(2,1)} %bitcast.50), channel_id=1, replica_groups=mesh['x'=4,'zl'=8,'zh'=2,'y'=4,'c'=2] {'zl'}, dimensions={0} | all-to-all | bytes 2097152 | tf_op jit(solution)/shard_map/all_to_all | solution.py:27
  62.2 0.9 convert_element_type.6
  63.1 45.3 %all_gather.10 = bf16[1,5,256,256]{3,2,1,0:T(8,128)(2,1)} all-gather(bf16[1,5,16,256]{3,2,1,0:T(8,128)(2,1)S(1)} %convert_element_type.6), channel_id=1, replica_groups=mesh['x'=4,'zl'=8,'zh'=2,'y'=4,'c'=2] {'zh','y','c'}, dimensions={2}, use_global_device_ids=true | all-gather | bytes 696320 | tf_op jit(solution)/shard_map/all_gather | solution.py:29
  108.5 0.7 fusion.7
  109.3 10.0 %all-gather.3.cloned.1.call-done = bf16[32,256,256]{2,1,0:T(8,128)(2,1)} async-done(((bf16[8,256,256]{2,1,0:T(8,128)(2,1)}), bf16[32,256,256]{2,1,0:T(8,128)(2,1)}) %all-gather.3.cloned.1.call-update) | async-done | bytes 4194320 | tf_op jit(solution)/shard_map/all_gather | solution.py:28
  119.3 6.7 %gather_fusion = bf16[40,256,256]{2,1,0:T(8,128)(2,1)} fusion(bf16[32,256,256]{2,1,0:T(8,128)(2,1)} %all-gather.3.cloned.1.call-done, s32[1024]{0:T(1024)S(1)} %pad_clamp_fusion.1), kind=kCustom, calls=%fused_computation | custom fusion | bytes 10485920 | tf_op jit(solution)/shard_map/gather | solution.py:33
  126.0 114.0 %all-gather.5.cloned.1.call-done = bf16[8,5,256,256]{3,2,1,0:T(8,128)(2,1)} async-done(((bf16[1,5,256,256]{3,2,1,0:T(8,128)(2,1)}), bf16[8,5,256,256]{3,2,1,0:T(8,128)(2,1)}) %all-gather.5.cloned.1.call-update) | async-done | bytes 5242896 | tf_op jit(solution)/shard_map/all_gather | solution.py:30
  240.0 12.5 %convolution_bitcast_fusion = f32[8,5,256,256]{2,3,1,0:T(8,128)} fusion(bf16[8,5,256,256]{3,2,1,0:T(8,128)(2,1)} %bitcast.46, bf16[8,5,256,256]{3,2,1,0:T(8,128)(2,1)} %all-gather.5.cloned.1.call-done), kind=kOutput, calls=%fused_computation.2 | convolution fusion | flops 2684878848 | bytes 20971520 | tf_op jit(solution)/shard_map/jtd,jktc->jkdc/dot_general | solution.py:37
  252.5 11.6 %copy.24 = f32[8,5,256,256]{3,0,1,2:T(8,128)} copy(f32[8,5,256,256]{2,3,1,0:T(8,128)} %convolution_bitcast_fusion) | data formatting | bytes 20971520 | tf_op jit(solution)/shard_map/jtd,jktc->jkdc/transpose | solution.py:37
  264.2 245.1 %reduce-scatter.3.cloned.1.call-done = f32[8,5,16,256]{3,0,1,2:T(8,128)} async-done(((f32[8,5,256,256]{3,0,1,2:T(8,128)}), f32[8,5,16,256]{3,0,1,2:T(8,128)}) %reduce-scatter.3.cloned.1.call-update) | async-done | bytes 655376 | tf_op jit(solution)/shard_map/reduce_scatter | solution.py:38
  509.3 2.1 copy.25
  511.5 0.7 iota_reduce_fusion
  512.2 58.2 %reduce-scatter.5.cloned.1.call-done = f32[1,5,16,256]{3,2,1,0:T(8,128)} async-done(((f32[8,5,16,256]{3,2,1,0:T(8,128)}), f32[1,5,16,256]{3,2,1,0:T(8,128)}) %reduce-scatter.5.cloned.1.call-update) | async-done | bytes 81936 | tf_op jit(solution)/shard_map/reduce_scatter | solution.py:39
  570.4 1.4 copy.26
  571.8 1.0 reshape.312
  572.8 14.2 %all-to-all-start.1 = ((f32[16,1,1280]{2,1,0:T(1,128)}), f32[16,1,1280]{2,1,0:T(1,128)S(1)}, u32[]{:S(2)}, u32[]{:S(2)}) async-start(f32[16,1,1280]{2,1,0:T(1,128)} %reshape.312), calls=%async_computation.3 | async-start | bytes 163840 | tf_op jit(solution)/shard_map/all_to_all | solution.py:40
  587.0 15.0 %all-to-all-done.1 = f32[16,1,1280]{2,1,0:T(1,128)S(1)} async-done(((f32[16,1,1280]{2,1,0:T(1,128)}), f32[16,1,1280]{2,1,0:T(1,128)S(1)}, u32[]{:S(2)}, u32[]{:S(2)}) %all-to-all-start.1) | async-done | bytes 81952 | tf_op jit(solution)/shard_map/all_to_all | solution.py:40
  602.0 0.5 broadcast.611
  602.5 0.8 reduce.19
  603.7 0.4 copy.32
  604.4 0.6 gather_fusion.1
  604.9 1.9 collective-permute-start
  606.9 13.1 %collective-permute-done = f32[5,16,256]{2,1,0:T(8,128)S(1)} collective-permute-done((f32[5,16,256]{2,1,0:T(8,128)S(1)}, f32[5,16,256]{2,1,0:T(8,128)S(1)}, u32[]{:S(2)}, u32[]{:S(2)}) %collective-permute-start) | collective-permute-done | bytes 81952 | tf_op jit(solution)/shard_map/ppermute | solution.py:48
  620.1 1.9 collective-permute-start.1
  622.0 12.3 %collective-permute-done.1 = f32[5,16,256]{2,1,0:T(8,128)S(1)} collective-permute-done((f32[5,16,256]{2,1,0:T(8,128)S(1)}, f32[5,16,256]{2,1,0:T(8,128)S(1)}, u32[]{:S(2)}, u32[]{:S(2)}) %collective-permute-start.1) | collective-permute-done | bytes 81952 | tf_op jit(solution)/shard_map/ppermute | solution.py:48
  634.3 1.9 collective-permute-start.2
  636.2 10.4 %collective-permute-done.2 = f32[5,16,256]{2,1,0:T(8,128)S(1)} collective-permute-done((f32[5,16,256]{2,1,0:T(8,128)S(1)}, f32[5,16,256]{2,1,0:T(8,128)S(1)}, u32[]{:S(2)}, u32[]{:S(2)}) %collective-permute-start.2) | collective-permute-done | bytes 81952 | tf_op jit(solution)/shard_map/ppermute | solution.py:48
  646.7 1.9 collective-permute-start.3
  648.7 5.6 collective-permute-done.3
  654.3 1.9 collective-permute-start.4
  656.3 5.8 collective-permute-done.4
  662.2 0.8 fusion.5
  (31 shorter events, 1.4 us)
Async XLA Ops:
  6.5 112.7 %all-gather.3.cloned.1.call-start = ((), (), s32[]{:S(2)}) async-start(), calls=%async_computation.4 | async-start | bytes 5242880 | tf_op jit(solution)/shard_map/all_gather | solution.py:28
  62.1 177.9 %all-gather.5.cloned.1.call-start = ((), (), s32[]{:S(2)}) async-start(), calls=%async_computation.5 | async-start | bytes 5898240 | tf_op jit(solution)/shard_map/all_gather | solution.py:30
  108.4 400.9 %reduce-scatter.3.cloned.1.call-start = ((), (), s32[]{:S(2)}) async-start(), calls=%async_computation.6 | async-start | bytes 11141120 | tf_op jit(solution)/shard_map/reduce_scatter | solution.py:38
  264.1 247.4 %copy-start.2 = (s32[1,5]{1,0:T(1,128)S(1)}, s32[1,5]{1,0:T(1,128)}, u32[]{:S(2)}) copy-start(s32[1,5]{1,0:T(1,128)} %param.5) | copy-start | bytes 64
  264.2 398.0 %copy-start.1 = (f32[1,5,16,256]{3,2,1,0:T(8,128)S(1)}, f32[1,5,16,256]{3,2,1,0:T(8,128)}, u32[]{:S(2)}) copy-start(f32[1,5,16,256]{3,2,1,0:T(8,128)} %param.4) | copy-start | bytes 245764
  264.2 306.2 %reduce-scatter.5.cloned.1.call-start = ((), (), s32[]{:S(2)}) async-start(), calls=%async_computation.7 | async-start | bytes 737280 | tf_op jit(solution)/shard_map/reduce_scatter | solution.py:39
  570.4 91.8 %copy-start = (f32[1,5,16,256]{3,2,1,0:T(8,128)S(1)}, f32[1,5,16,256]{3,2,1,0:T(8,128)}, u32[]{:S(2)}) copy-start(f32[1,5,16,256]{3,2,1,0:T(8,128)} %reduce-scatter.5.cloned.1.call-done) | copy-start | bytes 245764
  572.8 29.2 %all-to-all-start.1 = ((f32[16,1,1280]{2,1,0:T(1,128)}), f32[16,1,1280]{2,1,0:T(1,128)S(1)}, u32[]{:S(2)}, u32[]{:S(2)}) async-start(f32[16,1,1280]{2,1,0:T(1,128)} %reshape.312), calls=%async_computation.3 | async-start | bytes 163840 | tf_op jit(solution)/shard_map/all_to_all | solution.py:40
  604.9 15.0 %collective-permute-start = (f32[5,16,256]{2,1,0:T(8,128)S(1)}, f32[5,16,256]{2,1,0:T(8,128)S(1)}, u32[]{:S(2)}, u32[]{:S(2)}) collective-permute-start(f32[5,16,256]{2,1,0:T(8,128)S(1)} %gather_fusion.1), channel_id=1, source_target_pairs={{16,0},{32,16},{48,32},{64,48},{80,64},{96,80},{112,96},{128,112},... | collective-permute-start | bytes 245768 | tf_op jit(solution)/shard_map/ppermute | solution.py:48
  620.1 14.2 %collective-permute-start.1 = (f32[5,16,256]{2,1,0:T(8,128)S(1)}, f32[5,16,256]{2,1,0:T(8,128)S(1)}, u32[]{:S(2)}, u32[]{:S(2)}) collective-permute-start(f32[5,16,256]{2,1,0:T(8,128)S(1)} %broadcast_select_fusion), channel_id=1, source_target_pairs={{32,0},{48,16},{64,32},{80,48},{96,64},{112,80},{128,96},{144,112}... | collective-permute-start | bytes 245768 | tf_op jit(solution)/shard_map/ppermute | solution.py:48
  634.3 12.3 %collective-permute-start.2 = (f32[5,16,256]{2,1,0:T(8,128)S(1)}, f32[5,16,256]{2,1,0:T(8,128)S(1)}, u32[]{:S(2)}, u32[]{:S(2)}) collective-permute-start(f32[5,16,256]{2,1,0:T(8,128)S(1)} %broadcast_select_fusion.1), channel_id=1, source_target_pairs={{64,0},{80,16},{96,32},{112,48},{128,64},{144,80},{160,96},{176,11... | collective-permute-start | bytes 245768 | tf_op jit(solution)/shard_map/ppermute | solution.py:48
  646.7 7.5 %collective-permute-start.3 = (f32[5,16,256]{2,1,0:T(8,128)S(1)}, f32[5,16,256]{2,1,0:T(8,128)S(1)}, u32[]{:S(2)}, u32[]{:S(2)}) collective-permute-start(f32[5,16,256]{2,1,0:T(8,128)S(1)} %broadcast_select_fusion.2), channel_id=1, source_target_pairs={{128,0},{144,16},{160,32},{176,48},{192,64},{208,80},{224,96},{240... | collective-permute-start | bytes 245768 | tf_op jit(solution)/shard_map/ppermute | solution.py:48
  654.3 7.8 %collective-permute-start.4 = (f32[5,16,256]{2,1,0:T(8,128)S(1)}, f32[5,16,256]{2,1,0:T(8,128)S(1)}, u32[]{:S(2)}, u32[]{:S(2)}) collective-permute-start(f32[5,16,256]{2,1,0:T(8,128)S(1)} %broadcast_select_fusion.3), channel_id=1, source_target_pairs={{256,0},{272,16},{288,32},{304,48},{320,64},{336,80},{352,96},{368... | collective-permute-start | bytes 245768 | tf_op jit(solution)/shard_map/ppermute | solution.py:48
Sparse Core Ops, SparseCore 0:
  62.2 56.9 all-gather.2
  121.4 118.6 all-gather.4
  264.3 245.0 reduce-scatter.2
  512.3 58.1 reduce-scatter.4
where the time goes:
time: 670 us; the launch traced here: 669 us
  waiting for transfers between devices  490 us (73%)
  blocking collectives  101 us (15%)
  local copies, waits for them, and re-layouts  25 us (4%)
  starting transfers between devices  23.9 us (4%)
  between operations  13.3 us (2%)
  matrix products  12.5 us (2%)
    reduce_scatter x1, waiting for transfers between devices, per_device(): own_terms = lax.psum_scatter(left, REP, scatter_dimension=2, tiled=True)  245 us
    all_gather x1, waiting for transfers between devices, per_device(): panels = lax.all_gather(panels, 'zl', axis=0, tiled=True)  114 us
    reduce_scatter x1, waiting for transfers between devices, per_device(): lax.psum_scatter(own_terms, 'zl', scatter_dimension=0, tiled=True)[0]  58.2 us
    all_to_all x1, blocking collectives, per_device(): blocks = lax.all_to_all(own, 'zl', 0, 0, tiled=True)  55.6 us
    ppermute x5, waiting for transfers between devices, per_device(): shifted = lax.ppermute(outgoing, ('x', 'zl'), route)  47.2 us
    all_gather x1, blocking collectives, per_device(): panels = lax.all_gather(omega.astype(jnp.bfloat16), REP, axis=2, tiled=True)  45.3 us
    all_to_all x1, waiting for transfers between devices, per_device(): flipped = lax.all_to_all(own_terms, REP, 2, 1, tiled=True)  15 us
    all_to_all x1, starting transfers between devices, per_device(): flipped = lax.all_to_all(own_terms, REP, 2, 1, tiled=True)  14.2 us
  transfers between devices with their start and end apart: 10, of which 10 were waited for; matrix products, arithmetic and copies ran while one was open for 1% of the time, Pallas kernels for 0%

commit v1 on v0

--- a/solution.py
+++ b/solution.py
@@ -37,7 +37,10 @@
     left = jnp.einsum("jtd,jktc->jkdc", mixed, gathered, preferred_element_type=jnp.float32)
     own_terms = lax.psum_scatter(left, REP, scatter_dimension=2, tiled=True)
     own_terms = lax.psum_scatter(own_terms, "zl", scatter_dimension=0, tiled=True)[0]
-    flipped = lax.all_to_all(own_terms, REP, 2, 1, tiled=True)
+    flipped = jnp.concatenate(
+        lax.all_to_all(jnp.stack(jnp.split(own_terms, lax.axis_size(REP), axis=2)), REP, 0, 0),
+        axis=1,
+    )
     flipped = jnp.swapaxes(flipped, 1, 2)
     match = offsets[None, :] == jnp.mod(team_count - offsets, team_count)[:, None]
     mirror = jnp.argmax(match, axis=1)

time: 670 us -> 683 us (1.019)
  local copies, waits for them, and re-layouts: 25 us -> 37 us
    unnamed x8 -> x23, local copies, waits for them, and re-layouts: 1.32 us -> 13.9 us
where the time goes in v1:
time: 683 us; the launch traced here: 681 us
  waiting for transfers between devices  489 us (72%)
  blocking collectives  101 us (15%)
  local copies, waits for them, and re-layouts  37 us (5%)
  starting transfers between devices  23.9 us (3%)
  between operations  13.3 us (2%)
  matrix products  12.5 us (2%)
    reduce_scatter x1, waiting for transfers between devices, per_device(): own_terms = lax.psum_scatter(left, REP, scatter_dimension=2, tiled=True)  245 us
    all_gather x1, waiting for transfers between devices, per_device(): panels = lax.all_gather(panels, 'zl', axis=0, tiled=True)  114 us
    reduce_scatter x1, waiting for transfers between devices, per_device(): lax.psum_scatter(own_terms, 'zl', scatter_dimension=0, tiled=True)[0]  58.2 us
    all_to_all x1, blocking collectives, per_device(): blocks = lax.all_to_all(own, 'zl', 0, 0, tiled=True)  55.6 us
    ppermute x5, waiting for transfers between devices, per_device(): shifted = lax.ppermute(outgoing, ('x', 'zl'), route)  47.2 us
    all_gather x1, blocking collectives, per_device(): panels = lax.all_gather(omega.astype(jnp.bfloat16), REP, axis=2, tiled=True)  45.3 us
    all_to_all x1, waiting for transfers between devices, per_device(): lax.all_to_all(jnp.stack(jnp.split(own_terms, lax.axis_size(REP), axis=2)...  15 us
    all_to_all x1, starting transfers between devices, per_device(): lax.all_to_all(jnp.stack(jnp.split(own_terms, lax.axis_size(REP), axis=2)...  14.2 us
  transfers between devices with their start and end apart: 10, of which 10 were waited for; matrix products, arithmetic and copies ran while one was open for 1% of the time, Pallas kernels for 0%

profile of v1, /device:TPU:230, one launch (start us, length us, event | category | flops | bytes accessed | tf_op | source)
XLA Modules:
  0.0 681.4 jit_solution(17400444968461769958)
XLA Ops:
  6.5 55.6 %all_to_all.10 = bf16[8,256,256]{2,1,0:T(8,128)(2,1)} all-to-all(bf16[8,256,256]{2,1,0:T(8,128)(2,1)} %bitcast.123), channel_id=1, replica_groups=mesh['x'=4,'zl'=8,'zh'=2,'y'=4,'c'=2] {'zl'}, dimensions={0} | all-to-all | bytes 2097152 | tf_op jit(solution)/shard_map/all_to_all | solution.py:27
  62.2 0.9 convert_element_type.6
  63.1 45.3 %all_gather.10 = bf16[1,5,256,256]{3,2,1,0:T(8,128)(2,1)} all-gather(bf16[1,5,16,256]{3,2,1,0:T(8,128)(2,1)S(1)} %convert_element_type.6), channel_id=1, replica_groups=mesh['x'=4,'zl'=8,'zh'=2,'y'=4,'c'=2] {'zh','y','c'}, dimensions={2}, use_global_device_ids=true | all-gather | bytes 696320 | tf_op jit(solution)/shard_map/all_gather | solution.py:29
  109.3 10.0 %all-gather.3.cloned.1.call-done = bf16[32,256,256]{2,1,0:T(8,128)(2,1)} async-done(((bf16[8,256,256]{2,1,0:T(8,128)(2,1)}), bf16[32,256,256]{2,1,0:T(8,128)(2,1)}) %all-gather.3.cloned.1.call-update) | async-done | bytes 4194320 | tf_op jit(solution)/shard_map/all_gather | solution.py:28
  119.3 6.7 gather_fusion
  126.0 114.0 %all-gather.5.cloned.1.call-done = bf16[8,5,256,256]{3,2,1,0:T(8,128)(2,1)} async-done(((bf16[1,5,256,256]{3,2,1,0:T(8,128)(2,1)}), bf16[8,5,256,256]{3,2,1,0:T(8,128)(2,1)}) %all-gather.5.cloned.1.call-update) | async-done | bytes 5242896 | tf_op jit(solution)/shard_map/all_gather | solution.py:30
  240.0 12.5 %convolution_bitcast_fusion = f32[8,5,256,256]{2,3,1,0:T(8,128)} fusion(bf16[8,5,256,256]{3,2,1,0:T(8,128)(2,1)} %bitcast.105, bf16[8,5,256,256]{3,2,1,0:T(8,128)(2,1)} %all-gather.5.cloned.1.call-done), kind=kOutput, calls=%fused_computation.2 | convolution fusion | flops 2684878848 | bytes 20971520 | tf_op jit(solution)/shard_map/jtd,jktc->jkdc/dot_general | solution.py:37
  252.5 11.6 %copy.23 = f32[8,5,256,256]{3,0,1,2:T(8,128)} copy(f32[8,5,256,256]{2,3,1,0:T(8,128)} %convolution_bitcast_fusion) | data formatting | bytes 20971520 | tf_op jit(solution)/shard_map/jtd,jktc->jkdc/transpose | solution.py:37
  264.2 245.1 %reduce-scatter.3.cloned.1.call-done = f32[8,5,16,256]{3,0,1,2:T(8,128)} async-done(((f32[8,5,256,256]{3,0,1,2:T(8,128)}), f32[8,5,16,256]{3,0,1,2:T(8,128)}) %reduce-scatter.3.cloned.1.call-update) | async-done | bytes 655376 | tf_op jit(solution)/shard_map/reduce_scatter | solution.py:38
  509.3 2.1 copy.24
  512.2 58.2 %reduce-scatter.5.cloned.1.call-done = f32[1,5,16,256]{3,2,1,0:T(8,128)} async-done(((f32[8,5,16,256]{3,2,1,0:T(8,128)}), f32[1,5,16,256]{3,2,1,0:T(8,128)}) %reduce-scatter.5.cloned.1.call-update) | async-done | bytes 81936 | tf_op jit(solution)/shard_map/reduce_scatter | solution.py:39
  572.1 0.9 fusion.19
  573.0 0.9 fusion.18
  573.8 0.9 fusion.17
  574.7 0.9 fusion.16
  575.6 0.9 fusion.15
  579.8 0.9 fusion.10
  582.3 0.9 fusion.7
  583.2 0.9 fusion.6
  584.1 0.9 reshape.320
  585.0 14.2 %all-to-all-start.1 = ((f32[16,1,1280]{2,1,0:T(1,128)}), f32[16,1,1280]{2,1,0:T(1,128)S(1)}, u32[]{:S(2)}, u32[]{:S(2)}) async-start(f32[16,1,1280]{2,1,0:T(1,128)} %reshape.320), calls=%async_computation.3 | async-start | bytes 163840 | tf_op jit(solution)/shard_map/all_to_all | solution.py:41
  599.2 15.0 %all-to-all-done.1 = f32[16,1,1280]{2,1,0:T(1,128)S(1)} async-done(((f32[16,1,1280]{2,1,0:T(1,128)}), f32[16,1,1280]{2,1,0:T(1,128)S(1)}, u32[]{:S(2)}, u32[]{:S(2)}) %all-to-all-start.1) | async-done | bytes 81952 | tf_op jit(solution)/shard_map/all_to_all | solution.py:41
  616.9 1.9 collective-permute-start
  618.9 13.1 %collective-permute-done = f32[5,16,256]{2,1,0:T(8,128)S(1)} collective-permute-done((f32[5,16,256]{2,1,0:T(8,128)S(1)}, f32[5,16,256]{2,1,0:T(8,128)S(1)}, u32[]{:S(2)}, u32[]{:S(2)}) %collective-permute-start) | collective-permute-done | bytes 81952 | tf_op jit(solution)/shard_map/ppermute | solution.py:51
  632.0 1.9 collective-permute-start.1
  634.0 12.2 %collective-permute-done.1 = f32[5,16,256]{2,1,0:T(8,128)S(1)} collective-permute-done((f32[5,16,256]{2,1,0:T(8,128)S(1)}, f32[5,16,256]{2,1,0:T(8,128)S(1)}, u32[]{:S(2)}, u32[]{:S(2)}) %collective-permute-start.1) | collective-permute-done | bytes 81952 | tf_op jit(solution)/shard_map/ppermute | solution.py:51
  646.3 1.9 collective-permute-start.2
  648.2 10.4 %collective-permute-done.2 = f32[5,16,256]{2,1,0:T(8,128)S(1)} collective-permute-done((f32[5,16,256]{2,1,0:T(8,128)S(1)}, f32[5,16,256]{2,1,0:T(8,128)S(1)}, u32[]{:S(2)}, u32[]{:S(2)}) %collective-permute-start.2) | collective-permute-done | bytes 81952 | tf_op jit(solution)/shard_map/ppermute | solution.py:51
  658.7 1.9 collective-permute-start.3
  660.6 5.6 collective-permute-done.3
  666.3 1.9 collective-permute-start.4
  668.3 5.8 collective-permute-done.4
  (46 shorter events, 12.5 us)
Async XLA Ops:
  6.5 112.7 %all-gather.3.cloned.1.call-start = ((), (), s32[]{:S(2)}) async-start(), calls=%async_computation.4 | async-start | bytes 5242880 | tf_op jit(solution)/shard_map/all_gather | solution.py:28
  62.1 177.9 %all-gather.5.cloned.1.call-start = ((), (), s32[]{:S(2)}) async-start(), calls=%async_computation.5 | async-start | bytes 5898240 | tf_op jit(solution)/shard_map/all_gather | solution.py:30
  108.4 400.9 %reduce-scatter.3.cloned.1.call-start = ((), (), s32[]{:S(2)}) async-start(), calls=%async_computation.6 | async-start | bytes 11141120 | tf_op jit(solution)/shard_map/reduce_scatter | solution.py:38
  264.1 247.4 %copy-start.2 = (s32[1,5]{1,0:T(1,128)S(1)}, s32[1,5]{1,0:T(1,128)}, u32[]{:S(2)}) copy-start(s32[1,5]{1,0:T(1,128)} %param.5) | copy-start | bytes 64
  264.2 410.0 %copy-start.1 = (f32[1,5,16,256]{3,2,1,0:T(8,128)S(1)}, f32[1,5,16,256]{3,2,1,0:T(8,128)}, u32[]{:S(2)}) copy-start(f32[1,5,16,256]{3,2,1,0:T(8,128)} %param.4) | copy-start | bytes 245764
  264.2 306.2 %reduce-scatter.5.cloned.1.call-start = ((), (), s32[]{:S(2)}) async-start(), calls=%async_computation.7 | async-start | bytes 737280 | tf_op jit(solution)/shard_map/reduce_scatter | solution.py:39
  570.4 103.7 %copy-start = (f32[1,5,16,256]{3,2,1,0:T(8,128)S(1)}, f32[1,5,16,256]{3,2,1,0:T(8,128)}, u32[]{:S(2)}) copy-start(f32[1,5,16,256]{3,2,1,0:T(8,128)} %reduce-scatter.5.cloned.1.call-done) | copy-start | bytes 245764
  585.0 29.2 %all-to-all-start.1 = ((f32[16,1,1280]{2,1,0:T(1,128)}), f32[16,1,1280]{2,1,0:T(1,128)S(1)}, u32[]{:S(2)}, u32[]{:S(2)}) async-start(f32[16,1,1280]{2,1,0:T(1,128)} %reshape.320), calls=%async_computation.3 | async-start | bytes 163840 | tf_op jit(solution)/shard_map/all_to_all | solution.py:41
  616.9 15.0 %collective-permute-start = (f32[5,16,256]{2,1,0:T(8,128)S(1)}, f32[5,16,256]{2,1,0:T(8,128)S(1)}, u32[]{:S(2)}, u32[]{:S(2)}) collective-permute-start(f32[5,16,256]{2,1,0:T(8,128)S(1)} %gather_fusion.1), channel_id=1, source_target_pairs={{16,0},{32,16},{48,32},{64,48},{80,64},{96,80},{112,96},{128,112},... | collective-permute-start | bytes 245768 | tf_op jit(solution)/shard_map/ppermute | solution.py:51
  632.0 14.2 %collective-permute-start.1 = (f32[5,16,256]{2,1,0:T(8,128)S(1)}, f32[5,16,256]{2,1,0:T(8,128)S(1)}, u32[]{:S(2)}, u32[]{:S(2)}) collective-permute-start(f32[5,16,256]{2,1,0:T(8,128)S(1)} %broadcast_select_fusion), channel_id=1, source_target_pairs={{32,0},{48,16},{64,32},{80,48},{96,64},{112,80},{128,96},{144,112}... | collective-permute-start | bytes 245768 | tf_op jit(solution)/shard_map/ppermute | solution.py:51
  646.3 12.3 %collective-permute-start.2 = (f32[5,16,256]{2,1,0:T(8,128)S(1)}, f32[5,16,256]{2,1,0:T(8,128)S(1)}, u32[]{:S(2)}, u32[]{:S(2)}) collective-permute-start(f32[5,16,256]{2,1,0:T(8,128)S(1)} %broadcast_select_fusion.1), channel_id=1, source_target_pairs={{64,0},{80,16},{96,32},{112,48},{128,64},{144,80},{160,96},{176,11... | collective-permute-start | bytes 245768 | tf_op jit(solution)/shard_map/ppermute | solution.py:51
  658.7 7.5 %collective-permute-start.3 = (f32[5,16,256]{2,1,0:T(8,128)S(1)}, f32[5,16,256]{2,1,0:T(8,128)S(1)}, u32[]{:S(2)}, u32[]{:S(2)}) collective-permute-start(f32[5,16,256]{2,1,0:T(8,128)S(1)} %broadcast_select_fusion.2), channel_id=1, source_target_pairs={{128,0},{144,16},{160,32},{176,48},{192,64},{208,80},{224,96},{240... | collective-permute-start | bytes 245768 | tf_op jit(solution)/shard_map/ppermute | solution.py:51
  666.3 7.8 %collective-permute-start.4 = (f32[5,16,256]{2,1,0:T(8,128)S(1)}, f32[5,16,256]{2,1,0:T(8,128)S(1)}, u32[]{:S(2)}, u32[]{:S(2)}) collective-permute-start(f32[5,16,256]{2,1,0:T(8,128)S(1)} %broadcast_select_fusion.3), channel_id=1, source_target_pairs={{256,0},{272,16},{288,32},{304,48},{320,64},{336,80},{352,96},{368... | collective-permute-start | bytes 245768 | tf_op jit(solution)/shard_map/ppermute | solution.py:51
Sparse Core Ops, SparseCore 0:
  62.2 56.9 all-gather.2
  121.4 118.6 all-gather.4
  264.3 245.0 reduce-scatter.2
  512.3 58.1 reduce-scatter.4
